TPU v7x, 512 devices: a whole 4x4x16 slice. The times are simulated.
512 devices in a mesh: ctx: 8 (over x_hi, y), fsdp: 64 (over x_lo, z, core).
Axes of the slice: x: 4 (x_hi: 2, x_lo: 2; x = x_hi * 2 + x_lo), y: 4, z: 16, core: 2. Of those that a mesh axis runs over, the one named last changes fastest.
Arguments:
- hidden_rows: bfloat16 [64, 1024, 4608], P('fsdp', 'ctx'), may hold values from -6 to 6
- query_proj: bfloat16 [64, 1024, 2048], P('fsdp', 'ctx'), may hold values from -10 to 10
- key_proj: bfloat16 [64, 1024, 1024], P('fsdp', 'ctx'), may hold values from -10 to 10
- value_proj: bfloat16 [64, 1024, 1024], P('fsdp', 'ctx'), may hold values from -6 to 6
- order_pos: int32 [64, 1024], P('fsdp', 'ctx'), may hold values from 0 to 1023, each once within a row
- post_gain: float32 [4608], replicated, may hold values from 0.5 to 1.5
- out_weight: bfloat16 [2048, 4608], P('fsdp', 'ctx'), may hold values from -0.125 to 0.125
Outputs:
- residual_out: bfloat16 [64, 1024, 4608], P('fsdp', 'ctx')
Inputs may be any that keep to these rules, and one draw needn't show every extreme that they name: Each document's row of order_pos holds every position of 0 to 1023 exactly once.
All inputs are finite; a program needn't handle non-finite values.
Results may differ from a plain program's by a relative error of at most 0.0053.
Values may be sent and summed in bfloat16 or wider, within the bound.
A program may use at most 64 MiB of HBM per device.

v0:
```python
import jax
import jax.numpy as jnp
from jax import lax
from jax.sharding import PartitionSpec as P

HQ = 16
HK = 8
DH = 128
score_scale = 1.0 / 12.0
soft_cap = 50.0
norm_eps = 1e-06


def weigh_keys(query_heads, query_pos, key_heads, value_heads, key_pos):
    scores = (
        jnp.einsum("thgd,nhd->hgtn", query_heads, key_heads, preferred_element_type=jnp.float32)
        * score_scale
    )
    capped = soft_cap * jnp.tanh(scores / soft_cap)
    visible = key_pos[None, :] <= query_pos[:, None]
    weights = jnp.where(visible, jnp.exp(capped), 0.0)
    rounded = weights.astype(jnp.bfloat16)
    numerator = jnp.einsum(
        "hgtn,nhd->thgd", rounded, value_heads, preferred_element_type=jnp.float32
    )
    denominator = jnp.transpose(jnp.sum(weights, axis=-1), (2, 0, 1))
    return (numerator, denominator)


def shards(hidden_rows, query_proj, key_proj, value_proj, order_pos, post_gain, out_weight):
    tokens = query_proj.shape[1]
    groups = HQ // HK
    all_positions = lax.all_gather(order_pos, "ctx", axis=1, tiled=True)[0]
    weight_block = lax.all_gather(out_weight, "fsdp", axis=0, tiled=True)
    own_pos = order_pos[0]
    query_heads = query_proj[0].reshape(tokens, HK, groups, DH)
    key_piece = lax.all_gather(key_proj, "ctx", axis=1, tiled=True)
    value_piece = lax.all_gather(value_proj, "ctx", axis=1, tiled=True)
    piece_rows = key_piece.shape[1]
    numerator, denominator = weigh_keys(
        query_heads,
        own_pos,
        key_piece[0].reshape(piece_rows, HK, DH),
        value_piece[0].reshape(piece_rows, HK, DH),
        all_positions,
    )
    numerator, denominator = (numerator, denominator)
    attended = (numerator / denominator[..., None]).astype(jnp.bfloat16).reshape(1, tokens, HQ * DH)
    projected = jnp.dot(
        lax.all_gather(attended, "ctx", axis=1, tiled=True)[0],
        weight_block,
        preferred_element_type=jnp.float32,
    )
    token_rows = lax.all_to_all(
        projected.astype(jnp.bfloat16), "ctx", split_axis=0, concat_axis=1, tiled=True
    )
    widened = token_rows.astype(jnp.float32)
    normed = (
        widened
        * lax.rsqrt(jnp.mean(widened * widened, axis=-1, keepdims=True) + norm_eps)
        * post_gain
    )
    return (hidden_rows[0].astype(jnp.float32) + normed).astype(jnp.bfloat16)[None]


def solution(mesh):
    placed = (
        P("fsdp", "ctx", None),
        P("fsdp", "ctx", None),
        P("fsdp", "ctx", None),
        P("fsdp", "ctx", None),
        P("fsdp", "ctx"),
        P(),
        P("fsdp", "ctx"),
    )
    return jax.shard_map(
        shards, mesh=mesh, in_specs=placed, out_specs=P("fsdp", "ctx", None), check_vma=False
    )
```

profile of v0, /device:TPU:32, one launch (start us, length us, event | category | flops | bytes accessed | tf_op | source)
XLA Modules:
  0.0 404.5 jit_solution(9914539973454579862)
XLA Ops:
  6.5 0.0 all-gather.7.cloned.1.call-start
  6.5 0.7 all-gather.7.cloned.1.call-update
  7.3 0.0 all-gather.5.cloned.1.call-start
  7.3 1.8 copy.13
  9.1 0.0 all-gather.5.cloned.1.call-update
  9.1 0.0 all-gather.11.cloned.1.call-start
  9.2 0.7 all-gather.11.cloned.1.call-update
  9.9 0.0 all-gather.9.cloned.1.call-start
  9.9 1.4 reshape_squeeze.10
  11.3 23.6 %all_gather.15 = s32[1,1024]{1,0:T(1,128)S(1)} all-gather(s32[1,128]{1,0:T(1,128)} %param.11), channel_id=1, replica_groups=mesh['ctx'=8,'fsdp'=64] {'ctx'}, dimensions={1}, use_global_device_ids=true | all-gather | bytes 4608 | tf_op jit(solution)/shard_map/all_gather | solution.py:33
  34.9 0.9 broadcast_compare_fusion
  35.8 48.2 %all-gather.7.cloned.1.call-done = bf16[1,1024,1024]{2,1,0:T(8,128)(2,1)} async-done(((bf16[1,128,1024]{2,1,0:T(8,128)(2,1)}), bf16[1,1024,1024]{2,1,0:T(8,128)(2,1)}) %all-gather.7.cloned.1.call-update) | async-done | bytes 2097168 | tf_op jit(solution)/shard_map/all_gather | solution.py:38
  84.0 2.9 copy.16
  86.9 68.0 %all-gather.5.cloned.1.call-done = bf16[1,1024,1024]{1,2,0:T(8,128)(2,1)} async-done(((bf16[1,128,1024]{1,2,0:T(8,128)(2,1)}), bf16[1,1024,1024]{1,2,0:T(8,128)(2,1)}) %all-gather.5.cloned.1.call-update) | async-done | bytes 2097168 | tf_op jit(solution)/shard_map/all_gather | solution.py:37
  154.9 4.1 %fusion = (f32[8,2,128]{2,1,0:T(2,128)S(1)}, f32[8,1024,128,2]{2,1,3,0:T(8,128)S(1)}) fusion(pred[128,1024]{0,1:T(8,128)(4,1)S(1)} %broadcast_compare_fusion, bf16[1024,8,128,1]{0,2,3,1:T(8,128)(2,1)} %bitcast.60, bf16[128,8,2,128]{3,2,1,0:T(2,128)(2,1)S(1)} %reshape_squeeze.10), kind=kOutput, calls=%fused_computation.1 | convolution fusion | flops 545257472 | bytes 11149312 | tf_op jit(solution)/shard_map/thgd,nhd->hgtn/dot_general | solution.py:16
  159.0 3.4 divide_convert_fusion
  162.4 0.0 all-gather.9.cloned.1.call-update
  162.4 115.8 %all-gather.11.cloned.1.call-done = bf16[2048,576]{1,0:T(8,128)(2,1)} async-done(((bf16[32,576]{1,0:T(8,128)(2,1)}), bf16[2048,576]{1,0:T(8,128)(2,1)}) %all-gather.11.cloned.1.call-update) | async-done | bytes 2359312 | tf_op jit(solution)/shard_map/all_gather | solution.py:34
  278.3 88.1 %all-gather.9.cloned.1.call-done = bf16[1,1024,2048]{1,2,0:T(8,128)(2,1)} async-done(((bf16[1,128,2048]{1,2,0:T(8,128)(2,1)}), bf16[1,1024,2048]{1,2,0:T(8,128)(2,1)}) %all-gather.9.cloned.1.call-update) | async-done | bytes 4194320 | tf_op jit(solution)/shard_map/all_gather | solution.py:50
  366.4 5.7 %fusion.13 = bf16[72,8,8,128]{3,2,1,0:T(8,128)(2,1)S(1)} fusion(bf16[2048,576]{1,0:T(8,128)(2,1)} %all-gather.11.cloned.1.call-done, bf16[1,1024,2048]{1,2,0:T(8,128)(2,1)} %all-gather.9.cloned.1.call-done), kind=kOutput, calls=%fused_computation.13 | convolution fusion | flops 2416508928 | bytes 7733248 | tf_op jit(solution)/shard_map/dot_general | solution.py:49
  372.1 0.0 copy-start
  372.1 1.2 copy.31
  373.3 3.6 all-to-all-start
  376.9 0.0 copy-done
  376.9 0.7 copy.12
  377.7 0.0 copy-start.1
  377.7 16.1 %all-to-all-done = bf16[8,128,576]{1,2,0:T(8,128)(2,1)S(1)} async-done(((bf16[8,128,576]{1,2,0:T(8,128)(2,1)}), bf16[8,128,576]{1,2,0:T(8,128)(2,1)S(1)}, u32[]{:S(2)}, u32[]{:S(2)}) %all-to-all-start) | async-done | bytes 1179680 | tf_op jit(solution)/shard_map/all_to_all | solution.py:54
  393.8 0.6 multiply_reduce_fusion
  394.4 0.2 convert_element_type.47
  394.6 0.0 copy-done.1
  394.6 2.0 fusion.9
  396.6 1.4 copy.19
  (1 shorter events, 0.0 us)
Async XLA Ops:
  6.5 77.5 %all-gather.7.cloned.1.call-start = ((), (), s32[]{:S(2)}) async-start(), calls=%async_computation.2 | async-start | bytes 2359296 | tf_op jit(solution)/shard_map/all_gather | solution.py:38
  7.3 147.6 %all-gather.5.cloned.1.call-start = ((), (), s32[]{:S(2)}) async-start(), calls=%async_computation.1 | async-start | bytes 2359296 | tf_op jit(solution)/shard_map/all_gather | solution.py:37
  9.1 269.2 %all-gather.11.cloned.1.call-start = ((), (), s32[]{:S(2)}) async-start(), calls=%async_computation.4 | async-start | bytes 2662400 | tf_op jit(solution)/shard_map/all_gather | solution.py:34
  9.9 356.6 %all-gather.9.cloned.1.call-start = ((), (), s32[]{:S(2)}) async-start(), calls=%async_computation.3 | async-start | bytes 4718592 | tf_op jit(solution)/shard_map/all_gather | solution.py:50
  372.1 4.8 %copy-start = (bf16[1,128,4608]{2,1,0:T(8,128)(2,1)S(1)}, bf16[1,128,4608]{2,1,0:T(8,128)(2,1)}, u32[]{:S(2)}) copy-start(bf16[1,128,4608]{2,1,0:T(8,128)(2,1)} %param.7) | copy-start | bytes 3538948
  373.3 20.5 %all-to-all-start = ((bf16[8,128,576]{1,2,0:T(8,128)(2,1)}), bf16[8,128,576]{1,2,0:T(8,128)(2,1)S(1)}, u32[]{:S(2)}, u32[]{:S(2)}) async-start(bf16[8,128,576]{1,2,0:T(8,128)(2,1)} %bitcast.53), calls=%async_computation | async-start | bytes 2359296 | tf_op jit(solution)/shard_map/all_to_all | solution.py:54
  377.7 16.9 %copy-start.1 = (f32[4608]{0:T(1024)S(1)}, f32[4608]{0:T(1024)}, u32[]{:S(2)}) copy-start(f32[4608]{0:T(1024)} %param.12) | copy-start | bytes 55300
Sparse Core Ops, SparseCore 0:
  10.6 73.4 all-gather.6
  87.1 67.7 all-gather.4
  157.0 121.2 all-gather.10
  281.2 85.1 all-gather.8
where the time goes:
time: 405 us
  waiting for transfers between devices  338 us (83%)
  blocking collectives  23.6 us (6%)
  matrix products  13.2 us (3%)
  between operations  13.2 us (3%)
  local copies, waits for them, and re-layouts  9.43 us (2%)
    all_gather x1, waiting for transfers between devices, shards(): weight_block = lax.all_gather(out_weight, 'fsdp', axis=0, tiled=True)  116 us
    all_gather x1, waiting for transfers between devices, shards(): lax.all_gather(attended, 'ctx', axis=1, tiled=True)[0]  88.1 us
    all_gather x1, waiting for transfers between devices, shards(): key_piece = lax.all_gather(key_proj, 'ctx', axis=1, tiled=True)  68 us
    all_gather x1, waiting for transfers between devices, shards(): value_piece = lax.all_gather(value_proj, 'ctx', axis=1, tiled=True)  48.2 us
    all_gather x1, blocking collectives, shards(): all_positions = lax.all_gather(order_pos, 'ctx', axis=1, tiled=True)[0]  23.6 us
    all_to_all x1, waiting for transfers between devices, shards(): lax.all_to_all(projected.astype(jnp.bfloat16), 'ctx', split_axis=0, conca...  16.1 us
  transfers between devices with their start and end apart: 5, of which 5 were waited for; matrix products, arithmetic and copies ran while one was open for 4% of the time, Pallas kernels for 0%

commit v1 on v0

--- a/solution.py
+++ b/solution.py
@@ -9,6 +9,11 @@
 score_scale = 1.0 / 12.0
 soft_cap = 50.0
 norm_eps = 1e-06
+
+
+def swapped_in(x, mesh_axis, dim):
+    sent = jnp.stack([x] * lax.axis_size(mesh_axis))
+    return jnp.concatenate(lax.all_to_all(sent, mesh_axis, 0, 0), axis=dim)
 
 
 def weigh_keys(query_heads, query_pos, key_heads, value_heads, key_pos):
@@ -35,7 +40,7 @@
     own_pos = order_pos[0]
     query_heads = query_proj[0].reshape(tokens, HK, groups, DH)
     key_piece = lax.all_gather(key_proj, "ctx", axis=1, tiled=True)
-    value_piece = lax.all_gather(value_proj, "ctx", axis=1, tiled=True)
+    value_piece = swapped_in(value_proj, "ctx", 1)
     piece_rows = key_piece.shape[1]
     numerator, denominator = weigh_keys(
         query_heads,

time: 405 us -> 343 us (0.85)
  waiting for transfers between devices: 338 us -> 247 us
  blocking collectives: 23.6 us -> 42 us
  starting transfers between devices: 3.69 us -> 10.7 us
  local copies, waits for them, and re-layouts: 9.43 us -> 13.7 us
    all_gather x1 -> x0, waiting for transfers between devices: 48.2 us -> none  [shards(): value_piece = lax.all_gather(value_proj, 'ctx', axis=1, tiled=True)]
    all_gather x1, waiting for transfers between devices: 68 us -> 26.2 us  [shards(): key_piece = lax.all_gather(key_proj, 'ctx', axis=1, tiled=True)]
    all_gather x1, blocking collectives: 23.6 us -> 42 us  [shards(): all_positions = lax.all_gather(order_pos, 'ctx', axis=1, tiled=True)[0]]
    all_to_all x0 -> x1, starting transfers between devices: none -> 7.06 us  [swapped_in(): return jnp.concatenate(lax.all_to_all(sent, mesh_axis, 0, 0), axis=dim)]
    another operation x0 -> x3, local copies, waits for them, and re-layouts: none -> 5.53 us  [the longest x1 2.82 us: shards(): value_piece[0].reshape(piece_rows, HK, DH)]
  transfers between devices with their start and end apart: 5 -> 5, of which waited for: 5 -> 4; matrix products, arithmetic and copies ran while one was open for 4% -> 5% of each run, Pallas kernels for 0% -> 0%
where the time goes in v1:
time: 343 us
  waiting for transfers between devices  247 us (72%)
  blocking collectives  42 us (12%)
  local copies, waits for them, and re-layouts  13.7 us (4%)
  matrix products  13.2 us (4%)
  between operations  13.2 us (4%)
  starting transfers between devices  10.7 us (3%)
    all_gather x1, waiting for transfers between devices, shards(): weight_block = lax.all_gather(out_weight, 'fsdp', axis=0, tiled=True)  116 us
    all_gather x1, waiting for transfers between devices, shards(): lax.all_gather(attended, 'ctx', axis=1, tiled=True)[0]  88.3 us
    all_gather x1, blocking collectives, shards(): all_positions = lax.all_gather(order_pos, 'ctx', axis=1, tiled=True)[0]  42 us
    all_gather x1, waiting for transfers between devices, shards(): key_piece = lax.all_gather(key_proj, 'ctx', axis=1, tiled=True)  26.2 us
    all_to_all x1, waiting for transfers between devices, shards(): lax.all_to_all(projected.astype(jnp.bfloat16), 'ctx', split_axis=0, conca...  16.1 us
    all_to_all x1, starting transfers between devices, swapped_in(): return jnp.concatenate(lax.all_to_all(sent, mesh_axis, 0, 0), axis=dim)  7.06 us
  transfers between devices with their start and end apart: 5, of which 4 were waited for; matrix products, arithmetic and copies ran while one was open for 5% of the time, Pallas kernels for 0%

profile of v1, /device:TPU:32, one launch (start us, length us, event | category | flops | bytes accessed | tf_op | source)
XLA Modules:
  0.0 343.0 jit_solution(17960908994380285857)
XLA Ops:
  6.5 0.0 all-gather.4.cloned.1.call-start
  6.5 1.8 copy.21
  8.3 0.0 all-gather.4.cloned.1.call-update
  8.4 0.0 all-gather.8.cloned.1.call-start
  8.4 0.7 all-gather.8.cloned.1.call-update
  9.1 1.1 copy.24
  10.2 1.6 stack.2
  11.8 0.0 copy-start.1
  11.8 0.0 copy-start.3
  11.8 7.1 %all-to-all-start = ((bf16[8,1,128,1024]{2,3,1,0:T(8,128)(2,1)}), bf16[8,1,128,1024]{2,3,1,0:T(8,128)(2,1)S(1)}, u32[]{:S(2)}, u32[]{:S(2)}) async-start(bf16[8,1,128,1024]{2,3,1,0:T(8,128)(2,1)} %stack.2), calls=%async_computation | async-start | bytes 4194304 | tf_op jit(solution)/shard_map/all_to_all | solution.py:16
  18.9 0.0 all-gather.6.cloned.1.call-start
  18.9 0.0 copy-done.1
  18.9 0.4 reshape_squeeze.7
  19.3 0.0 copy-done.3
  19.3 42.0 %all_gather.12 = s32[1,1024]{1,0:T(1,128)S(1)} all-gather(s32[1,128]{1,0:T(1,128)S(1)} %copy-done.3), channel_id=1, replica_groups=mesh['ctx'=8,'fsdp'=64] {'ctx'}, dimensions={1}, use_global_device_ids=true | all-gather | bytes 4608 | tf_op jit(solution)/shard_map/all_gather | solution.py:38
  61.3 0.2 broadcast_compare_fusion
  61.5 0.0 all-to-all-done
  61.5 2.7 copy.25
  64.2 2.8 reshape.81
  67.0 26.2 %all-gather.4.cloned.1.call-done = bf16[1,1024,1024]{1,2,0:T(8,128)(2,1)} async-done(((bf16[1,128,1024]{1,2,0:T(8,128)(2,1)}), bf16[1,1024,1024]{1,2,0:T(8,128)(2,1)}) %all-gather.4.cloned.1.call-update) | async-done | bytes 2097168 | tf_op jit(solution)/shard_map/all_gather | solution.py:42
  93.2 4.1 %fusion = (f32[8,2,128]{2,1,0:T(2,128)S(1)}, f32[8,1024,128,2]{2,1,3,0:T(8,128)S(1)}) fusion(pred[128,1024]{0,1:T(8,128)(4,1)S(1)} %broadcast_compare_fusion, bf16[1024,8,128,1]{0,2,3,1:T(8,128)(2,1)} %bitcast.66, bf16[128,8,2,128]{3,2,1,0:T(2,128)(2,1)S(1)} %reshape_squeeze.7), kind=kOutput, calls=%fused_computation.1 | convolution fusion | flops 545257472 | bytes 11149312 | tf_op jit(solution)/shard_map/thgd,nhd->hgtn/dot_general | solution.py:21
  97.3 3.4 divide_convert_fusion
  100.7 0.0 all-gather.6.cloned.1.call-update
  100.8 115.8 %all-gather.8.cloned.1.call-done = bf16[2048,576]{1,0:T(8,128)(2,1)} async-done(((bf16[32,576]{1,0:T(8,128)(2,1)}), bf16[2048,576]{1,0:T(8,128)(2,1)}) %all-gather.8.cloned.1.call-update) | async-done | bytes 2359312 | tf_op jit(solution)/shard_map/all_gather | solution.py:39
  216.6 88.3 %all-gather.6.cloned.1.call-done = bf16[1,1024,2048]{1,2,0:T(8,128)(2,1)} async-done(((bf16[1,128,2048]{1,2,0:T(8,128)(2,1)}), bf16[1,1024,2048]{1,2,0:T(8,128)(2,1)}) %all-gather.6.cloned.1.call-update) | async-done | bytes 4194320 | tf_op jit(solution)/shard_map/all_gather | solution.py:55
  304.9 5.7 %fusion.14 = bf16[72,8,8,128]{3,2,1,0:T(8,128)(2,1)S(1)} fusion(bf16[2048,576]{1,0:T(8,128)(2,1)} %all-gather.8.cloned.1.call-done, bf16[1,1024,2048]{1,2,0:T(8,128)(2,1)} %all-gather.6.cloned.1.call-done), kind=kOutput, calls=%fused_computation.14 | convolution fusion | flops 2416508928 | bytes 7733248 | tf_op jit(solution)/shard_map/dot_general | solution.py:54
  310.6 0.0 copy-start
  310.6 1.2 copy.40
  311.8 3.6 %all-to-all-start.1 = ((bf16[8,128,576]{1,2,0:T(8,128)(2,1)}), bf16[8,128,576]{1,2,0:T(8,128)(2,1)S(1)}, u32[]{:S(2)}, u32[]{:S(2)}) async-start(bf16[8,128,576]{1,2,0:T(8,128)(2,1)} %bitcast.59), calls=%async_computation.1 | async-start | bytes 2359296 | tf_op jit(solution)/shard_map/all_to_all | solution.py:59
  315.4 0.0 copy-done
  315.4 0.7 copy.20
  316.1 0.0 copy-start.2
  316.1 16.1 %all-to-all-done.1 = bf16[8,128,576]{1,2,0:T(8,128)(2,1)S(1)} async-done(((bf16[8,128,576]{1,2,0:T(8,128)(2,1)}), bf16[8,128,576]{1,2,0:T(8,128)(2,1)S(1)}, u32[]{:S(2)}, u32[]{:S(2)}) %all-to-all-start.1) | async-done | bytes 1179680 | tf_op jit(solution)/shard_map/all_to_all | solution.py:59
  332.3 0.6 multiply_reduce_fusion
  332.9 0.2 convert_element_type.47
  333.1 0.0 copy-done.2
  333.1 2.0 fusion.9
  335.1 1.4 copy.28
  (1 shorter events, 0.0 us)
Async XLA Ops:
  6.5 86.6 %all-gather.4.cloned.1.call-start = ((), (), s32[]{:S(2)}) async-start(), calls=%async_computation.2 | async-start | bytes 2359296 | tf_op jit(solution)/shard_map/all_gather | solution.py:42
  8.4 208.2 %all-gather.8.cloned.1.call-start = ((), (), s32[]{:S(2)}) async-start(), calls=%async_computation.4 | async-start | bytes 2662400 | tf_op jit(solution)/shard_map/all_gather | solution.py:39
  11.8 7.1 %copy-start.1 = (bf16[1,128,2048]{2,1,0:T(8,128)(2,1)S(1)}, bf16[1,128,2048]{2,1,0:T(8,128)(2,1)}, u32[]{:S(2)}) copy-start(bf16[1,128,2048]{2,1,0:T(8,128)(2,1)} %param.8) | copy-start | bytes 1572868
  11.8 7.5 %copy-start.3 = (s32[1,128]{1,0:T(1,128)S(1)}, s32[1,128]{1,0:T(1,128)}, u32[]{:S(2)}) copy-start(s32[1,128]{1,0:T(1,128)} %param.11) | copy-start | bytes 1540
  11.8 49.7 %all-to-all-start = ((bf16[8,1,128,1024]{2,3,1,0:T(8,128)(2,1)}), bf16[8,1,128,1024]{2,3,1,0:T(8,128)(2,1)S(1)}, u32[]{:S(2)}, u32[]{:S(2)}) async-start(bf16[8,1,128,1024]{2,3,1,0:T(8,128)(2,1)} %stack.2), calls=%async_computation | async-start | bytes 4194304 | tf_op jit(solution)/shard_map/all_to_all | solution.py:16
  18.9 286.0 %all-gather.6.cloned.1.call-start = ((), (), s32[]{:S(2)}) async-start(), calls=%async_computation.3 | async-start | bytes 4718592 | tf_op jit(solution)/shard_map/all_gather | solution.py:55
  310.6 4.8 %copy-start = (bf16[1,128,4608]{2,1,0:T(8,128)(2,1)S(1)}, bf16[1,128,4608]{2,1,0:T(8,128)(2,1)}, u32[]{:S(2)}) copy-start(bf16[1,128,4608]{2,1,0:T(8,128)(2,1)} %param.7) | copy-start | bytes 3538948
  311.8 20.5 %all-to-all-start.1 = ((bf16[8,128,576]{1,2,0:T(8,128)(2,1)}), bf16[8,128,576]{1,2,0:T(8,128)(2,1)S(1)}, u32[]{:S(2)}, u32[]{:S(2)}) async-start(bf16[8,128,576]{1,2,0:T(8,128)(2,1)} %bitcast.59), calls=%async_computation.1 | async-start | bytes 2359296 | tf_op jit(solution)/shard_map/all_to_all | solution.py:59
  316.1 16.9 %copy-start.2 = (f32[4608]{0:T(1024)S(1)}, f32[4608]{0:T(1024)}, u32[]{:S(2)}) copy-start(f32[4608]{0:T(1024)} %param.12) | copy-start | bytes 55300
Sparse Core Ops, SparseCore 0:
  10.4 82.7 all-gather.3
  95.3 121.2 all-gather.7
  219.6 85.1 all-gather.5
